TPU v7x, 256 devices: a whole 4x4x8 slice. The times are simulated.
256 devices in a mesh: section: 8 (over y, core), dp: 32 (over z, x).
Axes of the slice: x: 4, y: 4, z: 8, core: 2. Of those that a mesh axis runs over, the one named last changes fastest.
Arguments:
- hidden_in: bfloat16 [4, 1024, 8192], P(None, 'dp'), may hold values from -6 to 6
- cotangent: bfloat16 [4, 1024, 8192], P(None, 'dp'), may hold values from -6 to 6
- adapter_in: bfloat16 [8, 8192, 128], P('section', 'dp'), may hold values from -0.0625 to 0.0625
- adapter_out: bfloat16 [8, 128, 8192], P('section', None, 'dp'), may hold values from -0.5 to 0.5
- norm_gain: bfloat16 [8, 8192], P('section', 'dp'), may hold values from 0.5 to 1.5
- user_of_row: int32 [4, 1024], P(None, 'dp'), may hold values from 0 to 63, as said below
- included: int32 [4, 64], P(None, 'dp'), may hold values 0 or 1
Outputs:
- grad_in: float32 [8, 8192, 128], P('section', 'dp')
- grad_out: float32 [8, 128, 8192], P('section', None, 'dp')
- user_weights: float32 [4, 64], P(None, 'dp')
Inputs may be any that keep to these rules, and one draw needn't show every extreme that they name: `user_of_row`: within one micro-batch, the rows of the j-th block of 32 rows belong to users j * 2 to j * 2 + 1, in rising order, each of them with one row or more.
All inputs are finite; a program needn't handle non-finite values. No bound on the sum of `included` on one device may be relied on, other than what follows from the above.
Results may differ from a plain program's by a relative error of at most 0.018.
Values may be sent and summed in bfloat16 or wider, within the bound.
A program may use at most 64 MiB of HBM per device.

v0:
```python
import math
import jax
import jax.numpy as jnp
from jax import lax
from jax.sharding import Mesh
from jax.sharding import PartitionSpec as P

DP = ("dp_0", "dp_1")


def gather_turned(arrays, axis, dims):
    turned = [jnp.moveaxis(a, dim, 0) for a, dim in zip(arrays, dims)]
    both = jnp.concatenate([t.reshape(len(t), -1) for t in turned], axis=1)
    result, at, done = (lax.all_gather(both, axis, axis=0, tiled=True), 0, [])
    for t, dim in zip(turned, dims):
        section = result[:, at : at + t[0].size].reshape(-1, *t.shape[1:])
        done.append(jnp.moveaxis(section, 0, dim))
        at += t[0].size
    return tuple(done)


def from_behind(block, axis, distance):
    devices = range(lax.axis_size(axis))
    route = [(i - distance, i) for i in devices if i - distance in devices]
    return lax.ppermute(block, axis, route)


def copy_for_each(x, axis):
    copies = jnp.broadcast_to(x, (lax.axis_size(axis), *x.shape))
    return lax.all_to_all(copies, axis, split_axis=0, concat_axis=0, tiled=True)


def taken_together(x, axis):
    return copy_for_each(x, axis).sum(axis=0)


def summed_rows(terms, axes):
    running = terms.astype(jnp.bfloat16)
    for axis in axes:
        running = lax.psum_scatter(running, axis, scatter_dimension=0, tiled=True)
    return running.astype(jnp.float32)


def normalize(stream_in, gain):
    stream = stream_in.astype(jnp.float32)
    scale = lax.rsqrt(jnp.mean(stream * stream, -1, keepdims=True) + 1e-05)
    unit = stream * scale
    normed = (unit * gain).astype(jnp.bfloat16)
    return (stream, scale, unit, normed)


def place(store, value, index, active):
    old = lax.dynamic_index_in_dim(store, index, 0, keepdims=False)
    return lax.dynamic_update_index_in_dim(store, jnp.where(active, value, old), index, 0)


def contract_last(left, right):
    return lax.dot_general(
        left, right, (((1,), (1,)), ((), ())), preferred_element_type=jnp.float32
    )


def contract_first(left, right):
    return lax.dot_general(
        left, right, (((0,), (0,)), ((), ())), preferred_element_type=jnp.float32
    )


def ghost(normed, err, low, delta, owners, onehot):
    same = owners[:, None] == owners[None, :]
    pairs = contract_last(normed, normed) * contract_last(err, err) + contract_last(
        low, low
    ) * contract_last(delta, delta)
    pairs = jnp.where(same, pairs, jnp.zeros_like(pairs))
    return jnp.sum(onehot * jnp.sum(pairs, -1)[:, None], 0)


def shards(hidden_in, cotangent, adapter_in, adapter_out, norm_gain, user_of_row, included):
    sections = lax.axis_size("section")
    section = lax.axis_index("section")
    dp_index = lax.axis_index(DP)
    a_full, b_full, g_full = gather_turned((adapter_in, adapter_out, norm_gain), DP, (1, 2, 1))
    a_mat = a_full[0]
    b_mat = b_full[0]
    gain = g_full[0].astype(jnp.float32)
    micro, rows, width = hidden_in.shape
    rank = a_mat.shape[1]
    users = included.shape[1]
    ticks = micro + sections - 1
    local_ids = user_of_row - dp_index * users
    onehot = (local_ids[:, :, None] == jnp.arange(users, dtype=jnp.int32)[None, None, :]).astype(
        jnp.float32
    )

    def forward_tick(carry, tick):
        incoming, keep_h, keep_n, keep_z = carry
        slot = tick - section
        active = (slot >= 0) & (slot < micro)
        index = jnp.clip(slot, 0, micro - 1)
        source = lax.dynamic_index_in_dim(hidden_in, index, 0, keepdims=False)
        current = jnp.where(section == 0, source, incoming)
        stream, scale, unit, normed = normalize(current, gain)
        low = jnp.dot(normed, a_mat, preferred_element_type=jnp.float32).astype(jnp.bfloat16)
        result = (stream + jnp.dot(low, b_mat, preferred_element_type=jnp.float32)).astype(
            jnp.bfloat16
        )
        keep_h = place(keep_h, current, index, active)
        keep_n = place(keep_n, normed, index, active)
        keep_z = place(keep_z, low, index, active)
        outgoing = from_behind(result, "section", 1)
        return ((outgoing, keep_h, keep_n, keep_z), None)

    start_fwd = (
        jnp.zeros((rows, width), jnp.bfloat16),
        jnp.zeros_like(hidden_in),
        jnp.zeros_like(hidden_in),
        jnp.zeros((micro, rows, rank), jnp.bfloat16),
    )
    (unused, keep_h, keep_n, keep_z), unused_out = lax.scan(
        forward_tick, start_fwd, jnp.arange(ticks, dtype=jnp.int32)
    )

    def backward_tick(carry, tick):
        incoming, carried, keep_e, keep_d, keep_p = carry
        slot = tick - (sections - 1 - section)
        active = (slot >= 0) & (slot < micro)
        index = jnp.clip(slot, 0, micro - 1)
        source = lax.dynamic_index_in_dim(cotangent, index, 0, keepdims=False)
        delta = jnp.where(section == sections - 1, source, incoming)
        current = lax.dynamic_index_in_dim(keep_h, index, 0, keepdims=False)
        normed = lax.dynamic_index_in_dim(keep_n, index, 0, keepdims=False)
        low = lax.dynamic_index_in_dim(keep_z, index, 0, keepdims=False)
        owners = lax.dynamic_index_in_dim(user_of_row, index, 0, keepdims=False)
        hot = lax.dynamic_index_in_dim(onehot, index, 0, keepdims=False)
        stream, scale, unit, unused_n = normalize(current, gain)
        err = contract_last(delta, b_mat).astype(jnp.bfloat16)
        slope = contract_last(err, a_mat) * gain
        grad_h = scale * (slope - unit * jnp.mean(slope * unit, -1, keepdims=True))
        previous = (delta.astype(jnp.float32) + grad_h).astype(jnp.bfloat16)
        partial_value = ghost(normed, err, low, delta, owners, hot)
        keep_e = place(keep_e, err, index, active)
        keep_d = place(keep_d, delta, index, active)
        keep_p = place(keep_p, partial_value, index, active)
        outgoing = from_behind(previous, "section", -1)
        return ((outgoing, carried, keep_e, keep_d, keep_p), None)

    start_bwd = (
        jnp.zeros((rows, width), jnp.bfloat16),
        jnp.zeros((users,), jnp.float32),
        jnp.zeros((micro, rows, rank), jnp.bfloat16),
        jnp.zeros_like(cotangent),
        jnp.zeros((micro, users), jnp.float32),
    )
    (unused_a, unused_b, keep_e, keep_d, keep_p), unused_out = lax.scan(
        backward_tick, start_bwd, jnp.arange(ticks, dtype=jnp.int32)
    )
    total = taken_together(keep_p, "section")
    bound = 0.8 * math.sqrt(sections * (rows // users) * width * width)
    user_weights = included.astype(jnp.float32) * (bound / jnp.maximum(jnp.sqrt(total), bound))
    row_weight = jnp.sum(onehot * user_weights[:, None, :], -1)[:, :, None]
    weighted_err = (
        (row_weight * keep_e.astype(jnp.float32)).astype(jnp.bfloat16).reshape(micro * rows, rank)
    )
    weighted_delta = (
        (row_weight * keep_d.astype(jnp.float32)).astype(jnp.bfloat16).reshape(micro * rows, width)
    )
    normed_rows = keep_n.reshape(micro * rows, width)
    low_rows = keep_z.reshape(micro * rows, rank)
    shard = summed_rows(
        jnp.concatenate(
            [contract_first(normed_rows, weighted_err), contract_first(weighted_delta, low_rows)], 1
        ),
        DP,
    )
    grad_in = shard[:, :rank]
    grad_out = shard[:, rank:].T
    return (grad_in[None], grad_out[None], user_weights)


def solution(mesh):
    torus = Mesh(mesh.devices.reshape(mesh.shape["section"], 8, 4), ("section", "dp_0", "dp_1"))
    return jax.shard_map(
        shards,
        mesh=torus,
        in_specs=(
            P(None, DP, None),
            P(None, DP, None),
            P("section", DP, None),
            P("section", None, DP),
            P("section", DP),
            P(None, DP),
            P(None, DP),
        ),
        out_specs=(P("section", DP, None), P("section", None, DP), P(None, DP)),
        check_vma=False,
    )
```

profile of v0, /device:TPU:8, one launch (start us, length us, event | category | flops | bytes accessed | tf_op | source)
XLA Modules:
  0.0 595.3 jit_solution(11264606444383854326)
XLA Ops:
  10.5 85.9 %all-gather.2.cloned.1.call-done = bf16[8192,257]{0,1:T(8,128)(2,1)} async-done(((bf16[256,257]{0,1:T(8,128)(2,1)}), bf16[8192,257]{0,1:T(8,128)(2,1)}) %all-gather.2.cloned.1.call-update) | async-done | bytes 4210704 | tf_op jit(solution)/shard_map/all_gather | solution.py:14
  96.3 3.9 slice_bitcast_fusion
  100.3 4.1 copy.19
  108.4 178.3 %while.35 = (s32[]{:T(128)}, bf16[32,8192]{1,0:T(8,128)(2,1)S(1)}, bf16[4,32,8192]{2,1,0:T(8,128)(2,1)}, bf16[4,32,8192]{2,1,0:T(8,128)(2,1)}, bf16[4,32,128]{2,...) while((s32[]{:T(128)}, bf16[32,8192]{1,0:T(8,128)(2,1)S(1)}, ...), condition=%wide.region_2.3_spmd, body=%wide.region_0.2_spmd.sunk | while | flops 138682400 | bytes 23185208 | solution.py:119
  118.2 6.4 %collective-permute-done = bf16[32,8192]{1,0:T(8,128)(2,1)S(1)} collective-permute-done((bf16[32,8192]{1,0:T(8,128)(2,1)S(1)}, bf16[32,8192]{1,0:T(8,128)(2,1)S(1)}, u32[]{:S(2)}, u32[]{:S(2)}) %collective-permute-start) | collective-permute-done | bytes 524320 | tf_op jit(solution)/shard_map/while/body/eval_jaxpr/ppermute | solution.py:25
  134.4 6.4 %collective-permute-done = bf16[32,8192]{1,0:T(8,128)(2,1)S(1)} collective-permute-done((bf16[32,8192]{1,0:T(8,128)(2,1)S(1)}, bf16[32,8192]{1,0:T(8,128)(2,1)S(1)}, u32[]{:S(2)}, u32[]{:S(2)}) %collective-permute-start) | collective-permute-done | bytes 524320 | tf_op jit(solution)/shard_map/while/body/eval_jaxpr/ppermute | solution.py:25
  150.6 6.4 %collective-permute-done = bf16[32,8192]{1,0:T(8,128)(2,1)S(1)} collective-permute-done((bf16[32,8192]{1,0:T(8,128)(2,1)S(1)}, bf16[32,8192]{1,0:T(8,128)(2,1)S(1)}, u32[]{:S(2)}, u32[]{:S(2)}) %collective-permute-start) | collective-permute-done | bytes 524320 | tf_op jit(solution)/shard_map/while/body/eval_jaxpr/ppermute | solution.py:25
  166.8 6.4 %collective-permute-done = bf16[32,8192]{1,0:T(8,128)(2,1)S(1)} collective-permute-done((bf16[32,8192]{1,0:T(8,128)(2,1)S(1)}, bf16[32,8192]{1,0:T(8,128)(2,1)S(1)}, u32[]{:S(2)}, u32[]{:S(2)}) %collective-permute-start) | collective-permute-done | bytes 524320 | tf_op jit(solution)/shard_map/while/body/eval_jaxpr/ppermute | solution.py:25
  183.0 6.4 %collective-permute-done = bf16[32,8192]{1,0:T(8,128)(2,1)S(1)} collective-permute-done((bf16[32,8192]{1,0:T(8,128)(2,1)S(1)}, bf16[32,8192]{1,0:T(8,128)(2,1)S(1)}, u32[]{:S(2)}, u32[]{:S(2)}) %collective-permute-start) | collective-permute-done | bytes 524320 | tf_op jit(solution)/shard_map/while/body/eval_jaxpr/ppermute | solution.py:25
  199.2 6.4 %collective-permute-done = bf16[32,8192]{1,0:T(8,128)(2,1)S(1)} collective-permute-done((bf16[32,8192]{1,0:T(8,128)(2,1)S(1)}, bf16[32,8192]{1,0:T(8,128)(2,1)S(1)}, u32[]{:S(2)}, u32[]{:S(2)}) %collective-permute-start) | collective-permute-done | bytes 524320 | tf_op jit(solution)/shard_map/while/body/eval_jaxpr/ppermute | solution.py:25
  215.5 6.4 %collective-permute-done = bf16[32,8192]{1,0:T(8,128)(2,1)S(1)} collective-permute-done((bf16[32,8192]{1,0:T(8,128)(2,1)S(1)}, bf16[32,8192]{1,0:T(8,128)(2,1)S(1)}, u32[]{:S(2)}, u32[]{:S(2)}) %collective-permute-start) | collective-permute-done | bytes 524320 | tf_op jit(solution)/shard_map/while/body/eval_jaxpr/ppermute | solution.py:25
  231.7 6.4 %collective-permute-done = bf16[32,8192]{1,0:T(8,128)(2,1)S(1)} collective-permute-done((bf16[32,8192]{1,0:T(8,128)(2,1)S(1)}, bf16[32,8192]{1,0:T(8,128)(2,1)S(1)}, u32[]{:S(2)}, u32[]{:S(2)}) %collective-permute-start) | collective-permute-done | bytes 524320 | tf_op jit(solution)/shard_map/while/body/eval_jaxpr/ppermute | solution.py:25
  247.9 6.4 %collective-permute-done = bf16[32,8192]{1,0:T(8,128)(2,1)S(1)} collective-permute-done((bf16[32,8192]{1,0:T(8,128)(2,1)S(1)}, bf16[32,8192]{1,0:T(8,128)(2,1)S(1)}, u32[]{:S(2)}, u32[]{:S(2)}) %collective-permute-start) | collective-permute-done | bytes 524320 | tf_op jit(solution)/shard_map/while/body/eval_jaxpr/ppermute | solution.py:25
  264.1 6.4 %collective-permute-done = bf16[32,8192]{1,0:T(8,128)(2,1)S(1)} collective-permute-done((bf16[32,8192]{1,0:T(8,128)(2,1)S(1)}, bf16[32,8192]{1,0:T(8,128)(2,1)S(1)}, u32[]{:S(2)}, u32[]{:S(2)}) %collective-permute-start) | collective-permute-done | bytes 524320 | tf_op jit(solution)/shard_map/while/body/eval_jaxpr/ppermute | solution.py:25
  280.3 6.4 %collective-permute-done = bf16[32,8192]{1,0:T(8,128)(2,1)S(1)} collective-permute-done((bf16[32,8192]{1,0:T(8,128)(2,1)S(1)}, bf16[32,8192]{1,0:T(8,128)(2,1)S(1)}, u32[]{:S(2)}, u32[]{:S(2)}) %collective-permute-start) | collective-permute-done | bytes 524320 | tf_op jit(solution)/shard_map/while/body/eval_jaxpr/ppermute | solution.py:25
  288.4 201.6 %while.36 = (s32[]{:T(128)}, bf16[32,8192]{1,0:T(8,128)(2,1)S(1)}, bf16[4,32,128]{2,1,0:T(8,128)(2,1)S(1)}, bf16[4,32,8192]{2,1,0:T(8,128)(2,1)}, f32[4,2]{1,0:T...) while((s32[]{:T(128)}, bf16[32,8192]{1,0:T(8,128)(2,1)S(1)}, ...), condition=%wide.region_8.9_spmd, body=%wide.region_3.8_spmd.sunk | while | flops 173029504 | bytes 33156040 | solution.py:154
  301.2 3.8 collective-permute-done.1
  308.6 2.2 bitcast_dynamic-update-slice_fusion.13
  313.0 3.8 collective-permute-start.1
  319.7 3.8 collective-permute-done.1
  331.5 3.8 collective-permute-start.1
  338.2 3.8 collective-permute-done.1
  350.0 3.8 collective-permute-start.1
  356.7 3.8 collective-permute-done.1
  364.1 2.2 bitcast_dynamic-update-slice_fusion.13
  368.5 3.8 collective-permute-start.1
  375.2 3.8 collective-permute-done.1
  382.6 2.2 bitcast_dynamic-update-slice_fusion.13
  387.0 3.8 collective-permute-start.1
  393.7 3.8 collective-permute-done.1
  405.5 3.8 collective-permute-start.1
  412.3 3.7 collective-permute-done.1
  424.0 3.8 collective-permute-start.1
  430.7 3.8 collective-permute-done.1
  438.1 2.2 bitcast_dynamic-update-slice_fusion.13
  442.5 3.8 collective-permute-start.1
  449.2 3.8 collective-permute-done.1
  456.6 2.2 bitcast_dynamic-update-slice_fusion.13
  461.0 3.8 collective-permute-start.1
  467.7 3.8 collective-permute-done.1
  475.1 2.2 bitcast_dynamic-update-slice_fusion.13
  479.5 3.8 collective-permute-start.1
  486.2 3.8 collective-permute-done.1
  490.1 9.5 %all_to_all.5 = f32[8,4,2]{1,2,0:T(2,128)S(1)} all-to-all(f32[8,4,2]{1,2,0:T(2,128)S(1)} %broadcast_in_dim.47), channel_id=1, replica_groups=mesh['section'=8,'dp_0'=8,'dp_1'=4] {'section'}, dimensions={0} | all-to-all | bytes 512 | tf_op jit(solution)/shard_map/all_to_all | solution.py:30
  499.9 2.6 fusion.28
  503.2 2.4 pad_maximum_fusion
  505.7 55.4 %reduce-scatter.3.cloned.1.call-done = bf16[1024,256]{0,1:T(8,128)(2,1)} async-done(((bf16[8192,256]{0,1:T(8,128)(2,1)}), bf16[1024,256]{0,1:T(8,128)(2,1)}) %reduce-scatter.3.cloned.1.call-update) | async-done | bytes 524304 | tf_op jit(solution)/shard_map/reduce_scatter | solution.py:40
  561.1 25.3 %reduce-scatter.5.cloned.1.call-done = bf16[256,256]{0,1:T(8,128)(2,1)} async-done(((bf16[1024,256]{0,1:T(8,128)(2,1)}), bf16[256,256]{0,1:T(8,128)(2,1)}) %reduce-scatter.5.cloned.1.call-update) | async-done | bytes 131088 | tf_op jit(solution)/shard_map/reduce_scatter | solution.py:40
  (417 shorter events, 212.9 us)
Async XLA Ops:
  7.2 89.2 %all-gather.2.cloned.1.call-start = ((), (), s32[]{:S(2)}) async-start(), calls=%async_computation.3 | async-start | bytes 4460544 | tf_op jit(solution)/shard_map/all_gather | solution.py:14
  9.7 551.3 %reduce-scatter.3.cloned.1.call-start = ((), (), s32[]{:S(2)}) async-start(), calls=%async_computation.4 | async-start | bytes 4718592 | tf_op jit(solution)/shard_map/reduce_scatter | solution.py:40
  109.6 3.6 copy-start
  114.1 10.5 %collective-permute-start = (bf16[32,8192]{1,0:T(8,128)(2,1)S(1)}, bf16[32,8192]{1,0:T(8,128)(2,1)S(1)}, u32[]{:S(2)}, u32[]{:S(2)}) collective-permute-start(bf16[32,8192]{1,0:T(8,128)(2,1)S(1)} %fusion.73), channel_id=1, source_target_pairs={{0,32},{32,64},{64,96},{96,128},{128,160},{160,192},{192,224},{1,3... | collective-permute-start | bytes 1572872 | tf_op jit(solution)/shard_map/while/body/eval_jaxpr/ppermute | solution.py:25
  125.8 3.6 copy-start
  130.3 10.5 %collective-permute-start = (bf16[32,8192]{1,0:T(8,128)(2,1)S(1)}, bf16[32,8192]{1,0:T(8,128)(2,1)S(1)}, u32[]{:S(2)}, u32[]{:S(2)}) collective-permute-start(bf16[32,8192]{1,0:T(8,128)(2,1)S(1)} %fusion.73), channel_id=1, source_target_pairs={{0,32},{32,64},{64,96},{96,128},{128,160},{160,192},{192,224},{1,3... | collective-permute-start | bytes 1572872 | tf_op jit(solution)/shard_map/while/body/eval_jaxpr/ppermute | solution.py:25
  142.0 3.6 copy-start
  146.5 10.5 %collective-permute-start = (bf16[32,8192]{1,0:T(8,128)(2,1)S(1)}, bf16[32,8192]{1,0:T(8,128)(2,1)S(1)}, u32[]{:S(2)}, u32[]{:S(2)}) collective-permute-start(bf16[32,8192]{1,0:T(8,128)(2,1)S(1)} %fusion.73), channel_id=1, source_target_pairs={{0,32},{32,64},{64,96},{96,128},{128,160},{160,192},{192,224},{1,3... | collective-permute-start | bytes 1572872 | tf_op jit(solution)/shard_map/while/body/eval_jaxpr/ppermute | solution.py:25
  158.2 3.6 copy-start
  162.7 10.5 %collective-permute-start = (bf16[32,8192]{1,0:T(8,128)(2,1)S(1)}, bf16[32,8192]{1,0:T(8,128)(2,1)S(1)}, u32[]{:S(2)}, u32[]{:S(2)}) collective-permute-start(bf16[32,8192]{1,0:T(8,128)(2,1)S(1)} %fusion.73), channel_id=1, source_target_pairs={{0,32},{32,64},{64,96},{96,128},{128,160},{160,192},{192,224},{1,3... | collective-permute-start | bytes 1572872 | tf_op jit(solution)/shard_map/while/body/eval_jaxpr/ppermute | solution.py:25
  174.4 3.6 copy-start
  178.9 10.5 %collective-permute-start = (bf16[32,8192]{1,0:T(8,128)(2,1)S(1)}, bf16[32,8192]{1,0:T(8,128)(2,1)S(1)}, u32[]{:S(2)}, u32[]{:S(2)}) collective-permute-start(bf16[32,8192]{1,0:T(8,128)(2,1)S(1)} %fusion.73), channel_id=1, source_target_pairs={{0,32},{32,64},{64,96},{96,128},{128,160},{160,192},{192,224},{1,3... | collective-permute-start | bytes 1572872 | tf_op jit(solution)/shard_map/while/body/eval_jaxpr/ppermute | solution.py:25
  190.7 3.6 copy-start
  195.1 10.5 %collective-permute-start = (bf16[32,8192]{1,0:T(8,128)(2,1)S(1)}, bf16[32,8192]{1,0:T(8,128)(2,1)S(1)}, u32[]{:S(2)}, u32[]{:S(2)}) collective-permute-start(bf16[32,8192]{1,0:T(8,128)(2,1)S(1)} %fusion.73), channel_id=1, source_target_pairs={{0,32},{32,64},{64,96},{96,128},{128,160},{160,192},{192,224},{1,3... | collective-permute-start | bytes 1572872 | tf_op jit(solution)/shard_map/while/body/eval_jaxpr/ppermute | solution.py:25
  206.9 3.6 copy-start
  211.4 10.5 %collective-permute-start = (bf16[32,8192]{1,0:T(8,128)(2,1)S(1)}, bf16[32,8192]{1,0:T(8,128)(2,1)S(1)}, u32[]{:S(2)}, u32[]{:S(2)}) collective-permute-start(bf16[32,8192]{1,0:T(8,128)(2,1)S(1)} %fusion.73), channel_id=1, source_target_pairs={{0,32},{32,64},{64,96},{96,128},{128,160},{160,192},{192,224},{1,3... | collective-permute-start | bytes 1572872 | tf_op jit(solution)/shard_map/while/body/eval_jaxpr/ppermute | solution.py:25
  223.1 3.6 copy-start
  227.6 10.5 %collective-permute-start = (bf16[32,8192]{1,0:T(8,128)(2,1)S(1)}, bf16[32,8192]{1,0:T(8,128)(2,1)S(1)}, u32[]{:S(2)}, u32[]{:S(2)}) collective-permute-start(bf16[32,8192]{1,0:T(8,128)(2,1)S(1)} %fusion.73), channel_id=1, source_target_pairs={{0,32},{32,64},{64,96},{96,128},{128,160},{160,192},{192,224},{1,3... | collective-permute-start | bytes 1572872 | tf_op jit(solution)/shard_map/while/body/eval_jaxpr/ppermute | solution.py:25
  239.3 3.6 copy-start
  243.8 10.5 %collective-permute-start = (bf16[32,8192]{1,0:T(8,128)(2,1)S(1)}, bf16[32,8192]{1,0:T(8,128)(2,1)S(1)}, u32[]{:S(2)}, u32[]{:S(2)}) collective-permute-start(bf16[32,8192]{1,0:T(8,128)(2,1)S(1)} %fusion.73), channel_id=1, source_target_pairs={{0,32},{32,64},{64,96},{96,128},{128,160},{160,192},{192,224},{1,3... | collective-permute-start | bytes 1572872 | tf_op jit(solution)/shard_map/while/body/eval_jaxpr/ppermute | solution.py:25
  255.5 3.6 copy-start
  260.0 10.5 %collective-permute-start = (bf16[32,8192]{1,0:T(8,128)(2,1)S(1)}, bf16[32,8192]{1,0:T(8,128)(2,1)S(1)}, u32[]{:S(2)}, u32[]{:S(2)}) collective-permute-start(bf16[32,8192]{1,0:T(8,128)(2,1)S(1)} %fusion.73), channel_id=1, source_target_pairs={{0,32},{32,64},{64,96},{96,128},{128,160},{160,192},{192,224},{1,3... | collective-permute-start | bytes 1572872 | tf_op jit(solution)/shard_map/while/body/eval_jaxpr/ppermute | solution.py:25
  271.7 3.6 copy-start
  276.2 10.5 %collective-permute-start = (bf16[32,8192]{1,0:T(8,128)(2,1)S(1)}, bf16[32,8192]{1,0:T(8,128)(2,1)S(1)}, u32[]{:S(2)}, u32[]{:S(2)}) collective-permute-start(bf16[32,8192]{1,0:T(8,128)(2,1)S(1)} %fusion.73), channel_id=1, source_target_pairs={{0,32},{32,64},{64,96},{96,128},{128,160},{160,192},{192,224},{1,3... | collective-permute-start | bytes 1572872 | tf_op jit(solution)/shard_map/while/body/eval_jaxpr/ppermute | solution.py:25
  288.4 211.3 %copy-start.5 = (s32[4,2]{0,1:T(2,128)S(1)}, s32[4,2]{0,1:T(2,128)}, u32[]{:S(2)}) copy-start(s32[4,2]{0,1:T(2,128)} %param.17) | copy-start | bytes 100
  296.4 8.6 %collective-permute-start.1 = (bf16[32,8192]{1,0:T(8,128)(2,1)S(1)}, bf16[32,8192]{1,0:T(8,128)(2,1)S(1)}, u32[]{:S(2)}, u32[]{:S(2)}) collective-permute-start(bf16[32,8192]{1,0:T(8,128)(2,1)S(1)} %fusion.86), channel_id=1, source_target_pairs={{32,0},{64,32},{96,64},{128,96},{160,128},{192,160},{224,192},{33,... | collective-permute-start | bytes 1572872 | tf_op jit(solution)/shard_map/while/body/eval_jaxpr/ppermute | solution.py:25
  308.6 3.1 copy-start.1
  308.6 3.1 copy-start.2
  313.0 10.5 %collective-permute-start.1 = (bf16[32,8192]{1,0:T(8,128)(2,1)S(1)}, bf16[32,8192]{1,0:T(8,128)(2,1)S(1)}, u32[]{:S(2)}, u32[]{:S(2)}) collective-permute-start(bf16[32,8192]{1,0:T(8,128)(2,1)S(1)} %fusion.86), channel_id=1, source_target_pairs={{32,0},{64,32},{96,64},{128,96},{160,128},{192,160},{224,192},{33,... | collective-permute-start | bytes 1572872 | tf_op jit(solution)/shard_map/while/body/eval_jaxpr/ppermute | solution.py:25
  331.5 10.5 %collective-permute-start.1 = (bf16[32,8192]{1,0:T(8,128)(2,1)S(1)}, bf16[32,8192]{1,0:T(8,128)(2,1)S(1)}, u32[]{:S(2)}, u32[]{:S(2)}) collective-permute-start(bf16[32,8192]{1,0:T(8,128)(2,1)S(1)} %fusion.86), channel_id=1, source_target_pairs={{32,0},{64,32},{96,64},{128,96},{160,128},{192,160},{224,192},{33,... | collective-permute-start | bytes 1572872 | tf_op jit(solution)/shard_map/while/body/eval_jaxpr/ppermute | solution.py:25
  350.0 10.5 %collective-permute-start.1 = (bf16[32,8192]{1,0:T(8,128)(2,1)S(1)}, bf16[32,8192]{1,0:T(8,128)(2,1)S(1)}, u32[]{:S(2)}, u32[]{:S(2)}) collective-permute-start(bf16[32,8192]{1,0:T(8,128)(2,1)S(1)} %fusion.86), channel_id=1, source_target_pairs={{32,0},{64,32},{96,64},{128,96},{160,128},{192,160},{224,192},{33,... | collective-permute-start | bytes 1572872 | tf_op jit(solution)/shard_map/while/body/eval_jaxpr/ppermute | solution.py:25
  364.1 3.1 copy-start.1
  364.1 3.1 copy-start.2
  368.5 10.5 %collective-permute-start.1 = (bf16[32,8192]{1,0:T(8,128)(2,1)S(1)}, bf16[32,8192]{1,0:T(8,128)(2,1)S(1)}, u32[]{:S(2)}, u32[]{:S(2)}) collective-permute-start(bf16[32,8192]{1,0:T(8,128)(2,1)S(1)} %fusion.86), channel_id=1, source_target_pairs={{32,0},{64,32},{96,64},{128,96},{160,128},{192,160},{224,192},{33,... | collective-permute-start | bytes 1572872 | tf_op jit(solution)/shard_map/while/body/eval_jaxpr/ppermute | solution.py:25
  382.6 3.1 copy-start.1
  387.0 10.5 %collective-permute-start.1 = (bf16[32,8192]{1,0:T(8,128)(2,1)S(1)}, bf16[32,8192]{1,0:T(8,128)(2,1)S(1)}, u32[]{:S(2)}, u32[]{:S(2)}) collective-permute-start(bf16[32,8192]{1,0:T(8,128)(2,1)S(1)} %fusion.86), channel_id=1, source_target_pairs={{32,0},{64,32},{96,64},{128,96},{160,128},{192,160},{224,192},{33,... | collective-permute-start | bytes 1572872 | tf_op jit(solution)/shard_map/while/body/eval_jaxpr/ppermute | solution.py:25
  405.5 10.5 %collective-permute-start.1 = (bf16[32,8192]{1,0:T(8,128)(2,1)S(1)}, bf16[32,8192]{1,0:T(8,128)(2,1)S(1)}, u32[]{:S(2)}, u32[]{:S(2)}) collective-permute-start(bf16[32,8192]{1,0:T(8,128)(2,1)S(1)} %fusion.86), channel_id=1, source_target_pairs={{32,0},{64,32},{96,64},{128,96},{160,128},{192,160},{224,192},{33,... | collective-permute-start | bytes 1572872 | tf_op jit(solution)/shard_map/while/body/eval_jaxpr/ppermute | solution.py:25
  424.0 10.5 %collective-permute-start.1 = (bf16[32,8192]{1,0:T(8,128)(2,1)S(1)}, bf16[32,8192]{1,0:T(8,128)(2,1)S(1)}, u32[]{:S(2)}, u32[]{:S(2)}) collective-permute-start(bf16[32,8192]{1,0:T(8,128)(2,1)S(1)} %fusion.86), channel_id=1, source_target_pairs={{32,0},{64,32},{96,64},{128,96},{160,128},{192,160},{224,192},{33,... | collective-permute-start | bytes 1572872 | tf_op jit(solution)/shard_map/while/body/eval_jaxpr/ppermute | solution.py:25
  438.1 3.1 copy-start.1
  438.1 3.1 copy-start.2
  442.5 10.4 %collective-permute-start.1 = (bf16[32,8192]{1,0:T(8,128)(2,1)S(1)}, bf16[32,8192]{1,0:T(8,128)(2,1)S(1)}, u32[]{:S(2)}, u32[]{:S(2)}) collective-permute-start(bf16[32,8192]{1,0:T(8,128)(2,1)S(1)} %fusion.86), channel_id=1, source_target_pairs={{32,0},{64,32},{96,64},{128,96},{160,128},{192,160},{224,192},{33,... | collective-permute-start | bytes 1572872 | tf_op jit(solution)/shard_map/while/body/eval_jaxpr/ppermute | solution.py:25
  456.6 3.1 copy-start.1
  456.6 3.1 copy-start.2
  461.0 10.5 %collective-permute-start.1 = (bf16[32,8192]{1,0:T(8,128)(2,1)S(1)}, bf16[32,8192]{1,0:T(8,128)(2,1)S(1)}, u32[]{:S(2)}, u32[]{:S(2)}) collective-permute-start(bf16[32,8192]{1,0:T(8,128)(2,1)S(1)} %fusion.86), channel_id=1, source_target_pairs={{32,0},{64,32},{96,64},{128,96},{160,128},{192,160},{224,192},{33,... | collective-permute-start | bytes 1572872 | tf_op jit(solution)/shard_map/while/body/eval_jaxpr/ppermute | solution.py:25
  475.1 3.1 copy-start.1
  475.1 3.1 copy-start.2
  479.5 10.5 %collective-permute-start.1 = (bf16[32,8192]{1,0:T(8,128)(2,1)S(1)}, bf16[32,8192]{1,0:T(8,128)(2,1)S(1)}, u32[]{:S(2)}, u32[]{:S(2)}) collective-permute-start(bf16[32,8192]{1,0:T(8,128)(2,1)S(1)} %fusion.86), channel_id=1, source_target_pairs={{32,0},{64,32},{96,64},{128,96},{160,128},{192,160},{224,192},{33,... | collective-permute-start | bytes 1572872 | tf_op jit(solution)/shard_map/while/body/eval_jaxpr/ppermute | solution.py:25
  505.6 80.7 %reduce-scatter.5.cloned.1.call-start = ((), (), s32[]{:S(2)}) async-start(), calls=%async_computation.5 | async-start | bytes 655360 | tf_op jit(solution)/shard_map/reduce_scatter | solution.py:40
  (13 other events, 39.1 us)
Sparse Core Ops, SparseCore 0:
  10.4 85.8 all-gather.1
  505.7 55.2 reduce-scatter.2
  563.6 22.7 reduce-scatter.4
where the time goes:
time: 599 us; the launch traced here: 595 us
  waiting for transfers between devices  279 us (47%)
  other arithmetic  87.2 us (15%)
  local copies, waits for them, and re-layouts  74 us (12%)
  starting transfers between devices  61.3 us (10%)
  matrix products  54.8 us (9%)
  loops' own time  15.8 us (3%)
  between operations  13.9 us (2%)
  blocking collectives  9.53 us (2%)
    ppermute x22, waiting for transfers between devices, from_behind(): return lax.ppermute(block, axis, route)  112 us
    all_gather x1, waiting for transfers between devices, gather_turned(): result, at, done = (lax.all_gather(both, axis, axis=0, tiled=True), 0, [])  85.9 us
    reduce_scatter x2, waiting for transfers between devices, summed_rows(): running = lax.psum_scatter(running, axis, scatter_dimension=0, tiled=True)  80.7 us
    ppermute x22, starting transfers between devices, from_behind(): return lax.ppermute(block, axis, route)  61.2 us
    dynamic_update_slice x33, other arithmetic, place(): lax.dynamic_update_index_in_dim(store, jnp.where(active, value, old), ind...  58.9 us
    dot_general x66, matrix products, contract_last(): lax.dot_general(left, right, (((1,), (1,)), ((), ())), preferred_element_...  41.6 us
    dynamic_slice x55, local copies, waits for them, and re-layouts, place(): old = lax.dynamic_index_in_dim(store, index, 0, keepdims=False)  37.5 us
    reduce_sum x22, other arithmetic, normalize(): scale = lax.rsqrt(jnp.mean(stream * stream, -1, keepdims=True) + 1e-05)  16.4 us
  transfers between devices with their start and end apart: 25, of which 25 were waited for; matrix products, arithmetic and copies ran while one was open for 9% of the time, Pallas kernels for 0%

commit v1 on v0

--- a/solution.py
+++ b/solution.py
@@ -8,10 +8,15 @@
 DP = ("dp_0", "dp_1")
 
 
+def all_by_exchange(value, mesh_axis, dim):
+    sent = jnp.stack([value] * lax.axis_size(mesh_axis))
+    return jnp.concatenate(lax.all_to_all(sent, mesh_axis, 0, 0), axis=dim)
+
+
 def gather_turned(arrays, axis, dims):
     turned = [jnp.moveaxis(a, dim, 0) for a, dim in zip(arrays, dims)]
     both = jnp.concatenate([t.reshape(len(t), -1) for t in turned], axis=1)
-    result, at, done = (lax.all_gather(both, axis, axis=0, tiled=True), 0, [])
+    result, at, done = (all_by_exchange(both, axis, 0), 0, [])
     for t, dim in zip(turned, dims):
         section = result[:, at : at + t[0].size].reshape(-1, *t.shape[1:])
         done.append(jnp.moveaxis(section, 0, dim))

time: 599 us -> 625 us (1.043)
  waiting for transfers between devices: 279 us -> 295 us
  starting transfers between devices: 61.3 us -> 72.8 us
    all_to_all x0 -> x1, waiting for transfers between devices: none -> 96.9 us  [all_by_exchange(): return jnp.concatenate(lax.all_to_all(sent, mesh_axis, 0, 0), axis=dim)]
    all_gather x1 -> x0, waiting for transfers between devices: 85.9 us -> none  [gather_turned(): result, at, done = (lax.all_gather(both, axis, axis=0, tiled=True), 0, [])]
    all_to_all x0 -> x1, starting transfers between devices: none -> 11.6 us  [all_by_exchange(): return jnp.concatenate(lax.all_to_all(sent, mesh_axis, 0, 0), axis=dim)]
    eq x11, local copies, waits for them, and re-layouts: 7.78 us -> 0.06 us  [ghost(): same = owners[:, None] == owners[None, :]]
    ppermute x22, waiting for transfers between devices: 112 us -> 120 us  [from_behind(): return lax.ppermute(block, axis, route)]
  transfers between devices with their start and end apart: 25 -> 25, of which waited for: 25 -> 25; matrix products, arithmetic and copies ran while one was open for 9% -> 8% of each run, Pallas kernels for 0% -> 0%
where the time goes in v1:
time: 625 us; the launch traced here: 622 us
  waiting for transfers between devices  295 us (47%)
  other arithmetic  84.9 us (14%)
  local copies, waits for them, and re-layouts  75 us (12%)
  starting transfers between devices  72.8 us (12%)
  matrix products  55.1 us (9%)
  loops' own time  15.3 us (2%)
  between operations  14.2 us (2%)
  blocking collectives  9.69 us (2%)
    ppermute x22, waiting for transfers between devices, from_behind(): return lax.ppermute(block, axis, route)  120 us
    all_to_all x1, waiting for transfers between devices, all_by_exchange(): return jnp.concatenate(lax.all_to_all(sent, mesh_axis, 0, 0), axis=dim)  96.9 us
    reduce_scatter x2, waiting for transfers between devices, summed_rows(): running = lax.psum_scatter(running, axis, scatter_dimension=0, tiled=True)  78.4 us
    ppermute x22, starting transfers between devices, from_behind(): return lax.ppermute(block, axis, route)  61.2 us
    dynamic_update_slice x33, other arithmetic, place(): lax.dynamic_update_index_in_dim(store, jnp.where(active, value, old), ind...  58.8 us
    dot_general x66, matrix products, contract_last(): lax.dot_general(left, right, (((1,), (1,)), ((), ())), preferred_element_...  41.9 us
    dynamic_slice x55, local copies, waits for them, and re-layouts, place(): old = lax.dynamic_index_in_dim(store, index, 0, keepdims=False)  37.5 us
    reduce_sum x22, other arithmetic, normalize(): scale = lax.rsqrt(jnp.mean(stream * stream, -1, keepdims=True) + 1e-05)  16.4 us
  transfers between devices with their start and end apart: 25, of which 25 were waited for; matrix products, arithmetic and copies ran while one was open for 8% of the time, Pallas kernels for 0%

profile of v1, /device:TPU:8, one launch (start us, length us, event | category | flops | bytes accessed | tf_op | source)
XLA Modules:
  0.0 621.9 jit_solution(3064682507843160051)
XLA Ops:
  9.0 2.3 stack.2
  11.3 11.6 %all-to-all-start = ((bf16[32,256,257]{1,2,0:T(8,128)(2,1)}), bf16[32,256,257]{1,2,0:T(8,128)(2,1)}, u32[]{:S(2)}, u32[]{:S(2)}) async-start(bf16[32,256,257]{1,2,0:T(8,128)(2,1)} %stack.2), calls=%async_computation | async-start | bytes 8650752 | tf_op jit(solution)/shard_map/all_to_all | solution.py:13
  22.9 96.9 %all-to-all-done = bf16[32,256,257]{1,2,0:T(8,128)(2,1)} async-done(((bf16[32,256,257]{1,2,0:T(8,128)(2,1)}), bf16[32,256,257]{1,2,0:T(8,128)(2,1)}, u32[]{:S(2)}, u32[]{:S(2)}) %all-to-all-start) | async-done | bytes 4210720 | tf_op jit(solution)/shard_map/all_to_all | solution.py:13
  119.9 3.2 copy.28
  123.5 5.1 copy.26
  130.3 4.1 copy.21
  137.5 177.8 %while.35 = (s32[]{:T(128)}, bf16[32,8192]{1,0:T(8,128)(2,1)S(1)}, bf16[4,32,8192]{2,1,0:T(8,128)(2,1)}, bf16[4,32,8192]{2,1,0:T(8,128)(2,1)}, bf16[4,32,128]{2,...) while((s32[]{:T(128)}, bf16[32,8192]{1,0:T(8,128)(2,1)S(1)}, ...), condition=%wide.region_2.3_spmd, body=%wide.region_0.2_spmd.sunk | while | flops 138682400 | bytes 23185208 | solution.py:124
  147.2 6.4 %collective-permute-done = bf16[32,8192]{1,0:T(8,128)(2,1)S(1)} collective-permute-done((bf16[32,8192]{1,0:T(8,128)(2,1)S(1)}, bf16[32,8192]{1,0:T(8,128)(2,1)S(1)}, u32[]{:S(2)}, u32[]{:S(2)}) %collective-permute-start) | collective-permute-done | bytes 524320 | tf_op jit(solution)/shard_map/while/body/eval_jaxpr/ppermute | solution.py:30
  163.4 6.4 %collective-permute-done = bf16[32,8192]{1,0:T(8,128)(2,1)S(1)} collective-permute-done((bf16[32,8192]{1,0:T(8,128)(2,1)S(1)}, bf16[32,8192]{1,0:T(8,128)(2,1)S(1)}, u32[]{:S(2)}, u32[]{:S(2)}) %collective-permute-start) | collective-permute-done | bytes 524320 | tf_op jit(solution)/shard_map/while/body/eval_jaxpr/ppermute | solution.py:30
  179.6 6.4 %collective-permute-done = bf16[32,8192]{1,0:T(8,128)(2,1)S(1)} collective-permute-done((bf16[32,8192]{1,0:T(8,128)(2,1)S(1)}, bf16[32,8192]{1,0:T(8,128)(2,1)S(1)}, u32[]{:S(2)}, u32[]{:S(2)}) %collective-permute-start) | collective-permute-done | bytes 524320 | tf_op jit(solution)/shard_map/while/body/eval_jaxpr/ppermute | solution.py:30
  195.7 6.4 %collective-permute-done = bf16[32,8192]{1,0:T(8,128)(2,1)S(1)} collective-permute-done((bf16[32,8192]{1,0:T(8,128)(2,1)S(1)}, bf16[32,8192]{1,0:T(8,128)(2,1)S(1)}, u32[]{:S(2)}, u32[]{:S(2)}) %collective-permute-start) | collective-permute-done | bytes 524320 | tf_op jit(solution)/shard_map/while/body/eval_jaxpr/ppermute | solution.py:30
  211.9 6.4 %collective-permute-done = bf16[32,8192]{1,0:T(8,128)(2,1)S(1)} collective-permute-done((bf16[32,8192]{1,0:T(8,128)(2,1)S(1)}, bf16[32,8192]{1,0:T(8,128)(2,1)S(1)}, u32[]{:S(2)}, u32[]{:S(2)}) %collective-permute-start) | collective-permute-done | bytes 524320 | tf_op jit(solution)/shard_map/while/body/eval_jaxpr/ppermute | solution.py:30
  228.1 6.4 %collective-permute-done = bf16[32,8192]{1,0:T(8,128)(2,1)S(1)} collective-permute-done((bf16[32,8192]{1,0:T(8,128)(2,1)S(1)}, bf16[32,8192]{1,0:T(8,128)(2,1)S(1)}, u32[]{:S(2)}, u32[]{:S(2)}) %collective-permute-start) | collective-permute-done | bytes 524320 | tf_op jit(solution)/shard_map/while/body/eval_jaxpr/ppermute | solution.py:30
  244.2 6.4 %collective-permute-done = bf16[32,8192]{1,0:T(8,128)(2,1)S(1)} collective-permute-done((bf16[32,8192]{1,0:T(8,128)(2,1)S(1)}, bf16[32,8192]{1,0:T(8,128)(2,1)S(1)}, u32[]{:S(2)}, u32[]{:S(2)}) %collective-permute-start) | collective-permute-done | bytes 524320 | tf_op jit(solution)/shard_map/while/body/eval_jaxpr/ppermute | solution.py:30
  260.4 6.4 %collective-permute-done = bf16[32,8192]{1,0:T(8,128)(2,1)S(1)} collective-permute-done((bf16[32,8192]{1,0:T(8,128)(2,1)S(1)}, bf16[32,8192]{1,0:T(8,128)(2,1)S(1)}, u32[]{:S(2)}, u32[]{:S(2)}) %collective-permute-start) | collective-permute-done | bytes 524320 | tf_op jit(solution)/shard_map/while/body/eval_jaxpr/ppermute | solution.py:30
  276.6 6.4 %collective-permute-done = bf16[32,8192]{1,0:T(8,128)(2,1)S(1)} collective-permute-done((bf16[32,8192]{1,0:T(8,128)(2,1)S(1)}, bf16[32,8192]{1,0:T(8,128)(2,1)S(1)}, u32[]{:S(2)}, u32[]{:S(2)}) %collective-permute-start) | collective-permute-done | bytes 524320 | tf_op jit(solution)/shard_map/while/body/eval_jaxpr/ppermute | solution.py:30
  292.7 6.4 %collective-permute-done = bf16[32,8192]{1,0:T(8,128)(2,1)S(1)} collective-permute-done((bf16[32,8192]{1,0:T(8,128)(2,1)S(1)}, bf16[32,8192]{1,0:T(8,128)(2,1)S(1)}, u32[]{:S(2)}, u32[]{:S(2)}) %collective-permute-start) | collective-permute-done | bytes 524320 | tf_op jit(solution)/shard_map/while/body/eval_jaxpr/ppermute | solution.py:30
  308.9 6.4 %collective-permute-done = bf16[32,8192]{1,0:T(8,128)(2,1)S(1)} collective-permute-done((bf16[32,8192]{1,0:T(8,128)(2,1)S(1)}, bf16[32,8192]{1,0:T(8,128)(2,1)S(1)}, u32[]{:S(2)}, u32[]{:S(2)}) %collective-permute-start) | collective-permute-done | bytes 524320 | tf_op jit(solution)/shard_map/while/body/eval_jaxpr/ppermute | solution.py:30
  316.9 201.5 %while.36 = (s32[]{:T(128)}, bf16[32,8192]{1,0:T(8,128)(2,1)S(1)}, bf16[4,32,128]{2,1,0:T(8,128)(2,1)S(1)}, bf16[4,32,8192]{2,1,0:T(8,128)(2,1)}, f32[4,2]{1,0:T...) while((s32[]{:T(128)}, bf16[32,8192]{1,0:T(8,128)(2,1)S(1)}, ...), condition=%wide.region_8.9_spmd, body=%wide.region_3.8_spmd.sunk | while | flops 173029504 | bytes 33156040 | solution.py:159
  329.1 4.5 collective-permute-done.1
  341.6 3.8 collective-permute-start.1
  347.6 4.5 collective-permute-done.1
  360.1 3.8 collective-permute-start.1
  366.1 4.5 collective-permute-done.1
  378.5 3.8 collective-permute-start.1
  384.6 4.5 collective-permute-done.1
  397.0 3.8 collective-permute-start.1
  403.1 4.5 collective-permute-done.1
  415.5 3.8 collective-permute-start.1
  421.6 4.5 collective-permute-done.1
  429.7 2.2 bitcast_dynamic-update-slice_fusion.13
  434.0 3.8 collective-permute-start.1
  440.1 4.4 collective-permute-done.1
  452.5 3.9 collective-permute-start.1
  458.6 4.5 collective-permute-done.1
  466.7 2.2 bitcast_dynamic-update-slice_fusion.13
  471.0 3.8 collective-permute-start.1
  477.1 4.4 collective-permute-done.1
  485.1 2.2 bitcast_dynamic-update-slice_fusion.13
  489.5 3.8 collective-permute-start.1
  495.6 4.4 collective-permute-done.1
  508.0 3.8 collective-permute-start.1
  514.1 4.4 collective-permute-done.1
  518.6 9.7 %all_to_all.10 = f32[8,4,2]{1,2,0:T(2,128)S(1)} all-to-all(f32[8,4,2]{1,2,0:T(2,128)S(1)} %broadcast_in_dim.47), channel_id=1, replica_groups=mesh['section'=8,'dp_0'=8,'dp_1'=4] {'section'}, dimensions={0} | all-to-all | bytes 512 | tf_op jit(solution)/shard_map/all_to_all | solution.py:35
  528.5 2.6 fusion.28
  531.9 2.4 pad_maximum_fusion
  534.3 53.0 %reduce-scatter.3.cloned.1.call-done = bf16[1024,256]{0,1:T(8,128)(2,1)} async-done(((bf16[8192,256]{0,1:T(8,128)(2,1)}), bf16[1024,256]{0,1:T(8,128)(2,1)}) %reduce-scatter.3.cloned.1.call-update) | async-done | bytes 524304 | tf_op jit(solution)/shard_map/reduce_scatter | solution.py:45
  587.4 25.3 %reduce-scatter.5.cloned.1.call-done = bf16[256,256]{0,1:T(8,128)(2,1)} async-done(((bf16[1024,256]{0,1:T(8,128)(2,1)}), bf16[256,256]{0,1:T(8,128)(2,1)}) %reduce-scatter.5.cloned.1.call-update) | async-done | bytes 131088 | tf_op jit(solution)/shard_map/reduce_scatter | solution.py:45
  (422 shorter events, 211.9 us)
Async XLA Ops:
  11.3 11.6 %copy-start.5 = (s32[4,32]{1,0:T(4,128)S(1)}, s32[4,32]{1,0:T(4,128)}, u32[]{:S(2)}) copy-start(s32[4,32]{1,0:T(4,128)} %param.16) | copy-start | bytes 1540
  11.3 108.6 %all-to-all-start = ((bf16[32,256,257]{1,2,0:T(8,128)(2,1)}), bf16[32,256,257]{1,2,0:T(8,128)(2,1)}, u32[]{:S(2)}, u32[]{:S(2)}) async-start(bf16[32,256,257]{1,2,0:T(8,128)(2,1)} %stack.2), calls=%async_computation | async-start | bytes 8650752 | tf_op jit(solution)/shard_map/all_to_all | solution.py:13
  22.8 564.5 %reduce-scatter.3.cloned.1.call-start = ((), (), s32[]{:S(2)}) async-start(), calls=%async_computation.4 | async-start | bytes 4718592 | tf_op jit(solution)/shard_map/reduce_scatter | solution.py:45
  138.7 3.6 copy-start
  143.2 10.5 %collective-permute-start = (bf16[32,8192]{1,0:T(8,128)(2,1)S(1)}, bf16[32,8192]{1,0:T(8,128)(2,1)S(1)}, u32[]{:S(2)}, u32[]{:S(2)}) collective-permute-start(bf16[32,8192]{1,0:T(8,128)(2,1)S(1)} %fusion.73), channel_id=1, source_target_pairs={{0,32},{32,64},{64,96},{96,128},{128,160},{160,192},{192,224},{1,3... | collective-permute-start | bytes 1572872 | tf_op jit(solution)/shard_map/while/body/eval_jaxpr/ppermute | solution.py:30
  154.9 3.6 copy-start
  159.3 10.5 %collective-permute-start = (bf16[32,8192]{1,0:T(8,128)(2,1)S(1)}, bf16[32,8192]{1,0:T(8,128)(2,1)S(1)}, u32[]{:S(2)}, u32[]{:S(2)}) collective-permute-start(bf16[32,8192]{1,0:T(8,128)(2,1)S(1)} %fusion.73), channel_id=1, source_target_pairs={{0,32},{32,64},{64,96},{96,128},{128,160},{160,192},{192,224},{1,3... | collective-permute-start | bytes 1572872 | tf_op jit(solution)/shard_map/while/body/eval_jaxpr/ppermute | solution.py:30
  171.0 3.6 copy-start
  175.5 10.5 %collective-permute-start = (bf16[32,8192]{1,0:T(8,128)(2,1)S(1)}, bf16[32,8192]{1,0:T(8,128)(2,1)S(1)}, u32[]{:S(2)}, u32[]{:S(2)}) collective-permute-start(bf16[32,8192]{1,0:T(8,128)(2,1)S(1)} %fusion.73), channel_id=1, source_target_pairs={{0,32},{32,64},{64,96},{96,128},{128,160},{160,192},{192,224},{1,3... | collective-permute-start | bytes 1572872 | tf_op jit(solution)/shard_map/while/body/eval_jaxpr/ppermute | solution.py:30
  187.2 3.6 copy-start
  191.7 10.5 %collective-permute-start = (bf16[32,8192]{1,0:T(8,128)(2,1)S(1)}, bf16[32,8192]{1,0:T(8,128)(2,1)S(1)}, u32[]{:S(2)}, u32[]{:S(2)}) collective-permute-start(bf16[32,8192]{1,0:T(8,128)(2,1)S(1)} %fusion.73), channel_id=1, source_target_pairs={{0,32},{32,64},{64,96},{96,128},{128,160},{160,192},{192,224},{1,3... | collective-permute-start | bytes 1572872 | tf_op jit(solution)/shard_map/while/body/eval_jaxpr/ppermute | solution.py:30
  203.3 3.6 copy-start
  207.8 10.5 %collective-permute-start = (bf16[32,8192]{1,0:T(8,128)(2,1)S(1)}, bf16[32,8192]{1,0:T(8,128)(2,1)S(1)}, u32[]{:S(2)}, u32[]{:S(2)}) collective-permute-start(bf16[32,8192]{1,0:T(8,128)(2,1)S(1)} %fusion.73), channel_id=1, source_target_pairs={{0,32},{32,64},{64,96},{96,128},{128,160},{160,192},{192,224},{1,3... | collective-permute-start | bytes 1572872 | tf_op jit(solution)/shard_map/while/body/eval_jaxpr/ppermute | solution.py:30
  219.5 3.6 copy-start
  224.0 10.5 %collective-permute-start = (bf16[32,8192]{1,0:T(8,128)(2,1)S(1)}, bf16[32,8192]{1,0:T(8,128)(2,1)S(1)}, u32[]{:S(2)}, u32[]{:S(2)}) collective-permute-start(bf16[32,8192]{1,0:T(8,128)(2,1)S(1)} %fusion.73), channel_id=1, source_target_pairs={{0,32},{32,64},{64,96},{96,128},{128,160},{160,192},{192,224},{1,3... | collective-permute-start | bytes 1572872 | tf_op jit(solution)/shard_map/while/body/eval_jaxpr/ppermute | solution.py:30
  235.7 3.6 copy-start
  240.1 10.5 %collective-permute-start = (bf16[32,8192]{1,0:T(8,128)(2,1)S(1)}, bf16[32,8192]{1,0:T(8,128)(2,1)S(1)}, u32[]{:S(2)}, u32[]{:S(2)}) collective-permute-start(bf16[32,8192]{1,0:T(8,128)(2,1)S(1)} %fusion.73), channel_id=1, source_target_pairs={{0,32},{32,64},{64,96},{96,128},{128,160},{160,192},{192,224},{1,3... | collective-permute-start | bytes 1572872 | tf_op jit(solution)/shard_map/while/body/eval_jaxpr/ppermute | solution.py:30
  251.8 3.6 copy-start
  256.3 10.5 %collective-permute-start = (bf16[32,8192]{1,0:T(8,128)(2,1)S(1)}, bf16[32,8192]{1,0:T(8,128)(2,1)S(1)}, u32[]{:S(2)}, u32[]{:S(2)}) collective-permute-start(bf16[32,8192]{1,0:T(8,128)(2,1)S(1)} %fusion.73), channel_id=1, source_target_pairs={{0,32},{32,64},{64,96},{96,128},{128,160},{160,192},{192,224},{1,3... | collective-permute-start | bytes 1572872 | tf_op jit(solution)/shard_map/while/body/eval_jaxpr/ppermute | solution.py:30
  268.0 3.6 copy-start
  272.5 10.5 %collective-permute-start = (bf16[32,8192]{1,0:T(8,128)(2,1)S(1)}, bf16[32,8192]{1,0:T(8,128)(2,1)S(1)}, u32[]{:S(2)}, u32[]{:S(2)}) collective-permute-start(bf16[32,8192]{1,0:T(8,128)(2,1)S(1)} %fusion.73), channel_id=1, source_target_pairs={{0,32},{32,64},{64,96},{96,128},{128,160},{160,192},{192,224},{1,3... | collective-permute-start | bytes 1572872 | tf_op jit(solution)/shard_map/while/body/eval_jaxpr/ppermute | solution.py:30
  284.2 3.6 copy-start
  288.6 10.5 %collective-permute-start = (bf16[32,8192]{1,0:T(8,128)(2,1)S(1)}, bf16[32,8192]{1,0:T(8,128)(2,1)S(1)}, u32[]{:S(2)}, u32[]{:S(2)}) collective-permute-start(bf16[32,8192]{1,0:T(8,128)(2,1)S(1)} %fusion.73), channel_id=1, source_target_pairs={{0,32},{32,64},{64,96},{96,128},{128,160},{160,192},{192,224},{1,3... | collective-permute-start | bytes 1572872 | tf_op jit(solution)/shard_map/while/body/eval_jaxpr/ppermute | solution.py:30
  300.3 3.6 copy-start
  304.8 10.5 %collective-permute-start = (bf16[32,8192]{1,0:T(8,128)(2,1)S(1)}, bf16[32,8192]{1,0:T(8,128)(2,1)S(1)}, u32[]{:S(2)}, u32[]{:S(2)}) collective-permute-start(bf16[32,8192]{1,0:T(8,128)(2,1)S(1)} %fusion.73), channel_id=1, source_target_pairs={{0,32},{32,64},{64,96},{96,128},{128,160},{160,192},{192,224},{1,3... | collective-permute-start | bytes 1572872 | tf_op jit(solution)/shard_map/while/body/eval_jaxpr/ppermute | solution.py:30
  316.9 211.4 %copy-start.6 = (s32[4,2]{0,1:T(2,128)S(1)}, s32[4,2]{0,1:T(2,128)}, u32[]{:S(2)}) copy-start(s32[4,2]{0,1:T(2,128)} %param.17) | copy-start | bytes 100
  320.6 3.1 copy-start.1
  320.6 3.1 copy-start.2
  325.0 8.6 %collective-permute-start.1 = (bf16[32,8192]{1,0:T(8,128)(2,1)S(1)}, bf16[32,8192]{1,0:T(8,128)(2,1)S(1)}, u32[]{:S(2)}, u32[]{:S(2)}) collective-permute-start(bf16[32,8192]{1,0:T(8,128)(2,1)S(1)} %fusion.86), channel_id=1, source_target_pairs={{32,0},{64,32},{96,64},{128,96},{160,128},{192,160},{224,192},{33,... | collective-permute-start | bytes 1572872 | tf_op jit(solution)/shard_map/while/body/eval_jaxpr/ppermute | solution.py:30
  341.6 10.5 %collective-permute-start.1 = (bf16[32,8192]{1,0:T(8,128)(2,1)S(1)}, bf16[32,8192]{1,0:T(8,128)(2,1)S(1)}, u32[]{:S(2)}, u32[]{:S(2)}) collective-permute-start(bf16[32,8192]{1,0:T(8,128)(2,1)S(1)} %fusion.86), channel_id=1, source_target_pairs={{32,0},{64,32},{96,64},{128,96},{160,128},{192,160},{224,192},{33,... | collective-permute-start | bytes 1572872 | tf_op jit(solution)/shard_map/while/body/eval_jaxpr/ppermute | solution.py:30
  360.1 10.5 %collective-permute-start.1 = (bf16[32,8192]{1,0:T(8,128)(2,1)S(1)}, bf16[32,8192]{1,0:T(8,128)(2,1)S(1)}, u32[]{:S(2)}, u32[]{:S(2)}) collective-permute-start(bf16[32,8192]{1,0:T(8,128)(2,1)S(1)} %fusion.86), channel_id=1, source_target_pairs={{32,0},{64,32},{96,64},{128,96},{160,128},{192,160},{224,192},{33,... | collective-permute-start | bytes 1572872 | tf_op jit(solution)/shard_map/while/body/eval_jaxpr/ppermute | solution.py:30
  378.5 10.5 %collective-permute-start.1 = (bf16[32,8192]{1,0:T(8,128)(2,1)S(1)}, bf16[32,8192]{1,0:T(8,128)(2,1)S(1)}, u32[]{:S(2)}, u32[]{:S(2)}) collective-permute-start(bf16[32,8192]{1,0:T(8,128)(2,1)S(1)} %fusion.86), channel_id=1, source_target_pairs={{32,0},{64,32},{96,64},{128,96},{160,128},{192,160},{224,192},{33,... | collective-permute-start | bytes 1572872 | tf_op jit(solution)/shard_map/while/body/eval_jaxpr/ppermute | solution.py:30
  397.0 10.5 %collective-permute-start.1 = (bf16[32,8192]{1,0:T(8,128)(2,1)S(1)}, bf16[32,8192]{1,0:T(8,128)(2,1)S(1)}, u32[]{:S(2)}, u32[]{:S(2)}) collective-permute-start(bf16[32,8192]{1,0:T(8,128)(2,1)S(1)} %fusion.86), channel_id=1, source_target_pairs={{32,0},{64,32},{96,64},{128,96},{160,128},{192,160},{224,192},{33,... | collective-permute-start | bytes 1572872 | tf_op jit(solution)/shard_map/while/body/eval_jaxpr/ppermute | solution.py:30
  415.5 10.5 %collective-permute-start.1 = (bf16[32,8192]{1,0:T(8,128)(2,1)S(1)}, bf16[32,8192]{1,0:T(8,128)(2,1)S(1)}, u32[]{:S(2)}, u32[]{:S(2)}) collective-permute-start(bf16[32,8192]{1,0:T(8,128)(2,1)S(1)} %fusion.86), channel_id=1, source_target_pairs={{32,0},{64,32},{96,64},{128,96},{160,128},{192,160},{224,192},{33,... | collective-permute-start | bytes 1572872 | tf_op jit(solution)/shard_map/while/body/eval_jaxpr/ppermute | solution.py:30
  429.6 3.1 copy-start.1
  429.7 3.1 copy-start.2
  434.0 10.5 %collective-permute-start.1 = (bf16[32,8192]{1,0:T(8,128)(2,1)S(1)}, bf16[32,8192]{1,0:T(8,128)(2,1)S(1)}, u32[]{:S(2)}, u32[]{:S(2)}) collective-permute-start(bf16[32,8192]{1,0:T(8,128)(2,1)S(1)} %fusion.86), channel_id=1, source_target_pairs={{32,0},{64,32},{96,64},{128,96},{160,128},{192,160},{224,192},{33,... | collective-permute-start | bytes 1572872 | tf_op jit(solution)/shard_map/while/body/eval_jaxpr/ppermute | solution.py:30
  452.5 10.5 %collective-permute-start.1 = (bf16[32,8192]{1,0:T(8,128)(2,1)S(1)}, bf16[32,8192]{1,0:T(8,128)(2,1)S(1)}, u32[]{:S(2)}, u32[]{:S(2)}) collective-permute-start(bf16[32,8192]{1,0:T(8,128)(2,1)S(1)} %fusion.86), channel_id=1, source_target_pairs={{32,0},{64,32},{96,64},{128,96},{160,128},{192,160},{224,192},{33,... | collective-permute-start | bytes 1572872 | tf_op jit(solution)/shard_map/while/body/eval_jaxpr/ppermute | solution.py:30
  466.6 3.1 copy-start.1
  466.7 3.1 copy-start.2
  471.0 10.5 %collective-permute-start.1 = (bf16[32,8192]{1,0:T(8,128)(2,1)S(1)}, bf16[32,8192]{1,0:T(8,128)(2,1)S(1)}, u32[]{:S(2)}, u32[]{:S(2)}) collective-permute-start(bf16[32,8192]{1,0:T(8,128)(2,1)S(1)} %fusion.86), channel_id=1, source_target_pairs={{32,0},{64,32},{96,64},{128,96},{160,128},{192,160},{224,192},{33,... | collective-permute-start | bytes 1572872 | tf_op jit(solution)/shard_map/while/body/eval_jaxpr/ppermute | solution.py:30
  485.1 3.1 copy-start.1
  485.1 3.1 copy-start.2
  489.5 10.5 %collective-permute-start.1 = (bf16[32,8192]{1,0:T(8,128)(2,1)S(1)}, bf16[32,8192]{1,0:T(8,128)(2,1)S(1)}, u32[]{:S(2)}, u32[]{:S(2)}) collective-permute-start(bf16[32,8192]{1,0:T(8,128)(2,1)S(1)} %fusion.86), channel_id=1, source_target_pairs={{32,0},{64,32},{96,64},{128,96},{160,128},{192,160},{224,192},{33,... | collective-permute-start | bytes 1572872 | tf_op jit(solution)/shard_map/while/body/eval_jaxpr/ppermute | solution.py:30
  503.6 3.1 copy-start.1
  503.6 3.1 copy-start.2
  508.0 10.5 %collective-permute-start.1 = (bf16[32,8192]{1,0:T(8,128)(2,1)S(1)}, bf16[32,8192]{1,0:T(8,128)(2,1)S(1)}, u32[]{:S(2)}, u32[]{:S(2)}) collective-permute-start(bf16[32,8192]{1,0:T(8,128)(2,1)S(1)} %fusion.86), channel_id=1, source_target_pairs={{32,0},{64,32},{96,64},{128,96},{160,128},{192,160},{224,192},{33,... | collective-permute-start | bytes 1572872 | tf_op jit(solution)/shard_map/while/body/eval_jaxpr/ppermute | solution.py:30
  534.3 78.4 %reduce-scatter.5.cloned.1.call-start = ((), (), s32[]{:S(2)}) async-start(), calls=%async_computation.5 | async-start | bytes 655360 | tf_op jit(solution)/shard_map/reduce_scatter | solution.py:45
  (14 other events, 42.2 us)
Sparse Core Ops, SparseCore 0:
  534.4 52.9 reduce-scatter.2
  589.9 22.7 reduce-scatter.4
